TPU v7x, 512 devices: a whole 4x8x8 slice. The times are simulated.
512 devices in a mesh: dp: 16 (over z, core), expert: 32 (over x, y).
Axes of the slice: x: 4, y: 8, z: 8, core: 2. Of those that a mesh axis runs over, the one named last changes fastest.
Arguments:
- pivot_states: bfloat16 [65536, 2048], P(('dp', 'expert')), may hold values from -6 to 6
- queries: bfloat16 [65536, 2048], P(('dp', 'expert')), may hold values from -8 to 8
- keys: bfloat16 [65536, 2048], P(('dp', 'expert')), may hold values from -8 to 8
- values: bfloat16 [65536, 2048], P(('dp', 'expert')), may hold values from -6 to 6
- pack_pos: int32 [65536], P(('dp', 'expert')), may hold values from 0 to 2047, as said below
- segment_ids: int32 [512, 128], P(('dp', 'expert')), may hold values from 0 to 7, never falling along the last dimension, each value on 1 to 64 neighbouring positions
- expert_ids: int32 [65536, 2], P(('dp', 'expert')), may hold values from 0 to 127, all different within a row
- gate_code: int32 [65536, 2], P(('dp', 'expert')), may hold values from 6554 to 65535
- ln_gain: float32 [2048], replicated, may hold values from 0.5 to 1.5
- ln_bias: float32 [2048], replicated, may hold values from -3 to 3
- w_in: bfloat16 [32, 2048, 4096], P('expert', None, 'dp'), may hold values from -0.125 to 0.125
- b_in: float32 [32, 4096], P('expert', 'dp'), may hold values from -3 to 3
- w_out: bfloat16 [32, 4096, 2048], P('expert', 'dp'), may hold values from -0.09375 to 0.09375
- b_out: float32 [32, 2048], replicated, may hold values from -3 to 3
Outputs:
- layer_out: bfloat16 [65536, 2048], P(('dp', 'expert'))
Inputs may be any that keep to these rules, and one draw needn't show every extreme that they name: Within one index of expert, pack_pos over the devices of dp is a permutation, and each device's tokens go exactly 8 to each packed block of its column. `expert_ids`: only ids below 32 belong to the experts of this round.
All inputs are finite; a program needn't handle non-finite values.
Results may differ from a plain program's by a relative error of at most 0.0055.
Values may be sent and summed in bfloat16 or wider, within the bound.
A program may use at most 64 MiB of HBM per device.

v0:
```python
import math
import jax
import jax.numpy as jnp
from jax import lax
from jax.sharding import PartitionSpec as P

HEAD_DIM = 128
ROUNDS = 4
epsilon = 1e-05
mask_fill = -1e30


def per_device(
    pivot_states,
    queries,
    keys,
    values,
    pack_pos,
    segment_ids,
    expert_ids,
    gate_code,
    ln_gain,
    ln_bias,
    w_in,
    b_in,
    w_out,
    b_out,
):
    tok_count = pivot_states.shape[0]
    model_width = pivot_states.shape[1]
    dp_count = lax.axis_size("dp")
    expert_count = lax.axis_size("expert")
    per_target = tok_count // dp_count
    target_block = pack_pos // tok_count
    offsets = pack_pos % tok_count
    target_hot = (target_block[:, None] == jnp.arange(dp_count, dtype=jnp.int32)[None, :]).astype(
        jnp.int32
    )
    bucket_rank = jnp.sum(jnp.cumsum(target_hot, axis=0) * target_hot, axis=1) - 1
    send_index = target_block * per_target + bucket_rank
    joined = jnp.concatenate([pivot_states, queries, keys, values], axis=1)
    send_rows = jnp.zeros_like(joined).at[send_index].set(joined)
    send_offsets = jnp.zeros_like(offsets).at[send_index].set(offsets)
    recv_rows, recv_offsets = (
        lax.all_to_all(send_rows, "dp", split_axis=0, concat_axis=0, tiled=True),
        lax.all_to_all(send_offsets, "dp", split_axis=0, concat_axis=0, tiled=True),
    )
    packed = jnp.zeros_like(recv_rows).at[recv_offsets].set(recv_rows)
    state_rows = packed[:, :model_width]
    query_rows = packed[:, model_width : 2 * model_width]
    key_rows = packed[:, 2 * model_width : 3 * model_width]
    value_rows = packed[:, 3 * model_width :]
    head_count = model_width // HEAD_DIM
    key_heads = key_rows.reshape(tok_count, head_count, HEAD_DIM)
    value_heads = value_rows.reshape(tok_count, head_count, HEAD_DIM)
    seg_row = segment_ids[0]
    block_rows = min(tok_count, 512)
    block_count = tok_count // block_rows
    score_scale = 1.0 / math.sqrt(HEAD_DIM)

    def attend(block_args):
        query_block, seg_block = block_args
        query_heads = query_block.reshape(block_rows, head_count, HEAD_DIM)
        scores = (
            jnp.einsum("qhd,khd->hqk", query_heads, key_heads, preferred_element_type=jnp.float32)
            * score_scale
        )
        same_doc = seg_block[:, None] == seg_row[None, :]
        scores = jnp.where(same_doc[None, :, :], scores, mask_fill)
        top_score = jnp.max(scores, axis=2, keepdims=True)
        exp_terms = jnp.exp(scores - top_score)
        softmax_weights = (exp_terms / jnp.sum(exp_terms, axis=2, keepdims=True)).astype(
            jnp.bfloat16
        )
        mixed_heads = jnp.einsum(
            "hqk,khd->qhd", softmax_weights, value_heads, preferred_element_type=jnp.float32
        )
        return mixed_heads.reshape(block_rows, model_width)

    attended = lax.map(
        attend,
        (
            query_rows.reshape(block_count, block_rows, model_width),
            seg_row.reshape(block_count, block_rows),
        ),
    )
    hidden_state = state_rows.astype(jnp.float32) + attended.reshape(tok_count, model_width)
    mean_value = jnp.mean(hidden_state, axis=1, keepdims=True)
    centered = hidden_state - mean_value
    variance = jnp.mean(centered * centered, axis=1, keepdims=True)
    normed = (centered * lax.rsqrt(variance + epsilon) * ln_gain + ln_bias).astype(jnp.bfloat16)
    capacity = max(2, 2 * tok_count // (ROUNDS * expert_count))
    assigned = jnp.concatenate([expert_ids[:, 0], expert_ids[:, 1]])
    expert_hot = (assigned[:, None] == jnp.arange(expert_count, dtype=jnp.int32)[None, :]).astype(
        jnp.int32
    )
    slot_rank = jnp.sum(jnp.cumsum(expert_hot, axis=0) * expert_hot, axis=1) - 1
    kept_mask = (assigned < expert_count) & (slot_rank < capacity)
    overflow = expert_count * capacity
    slot_index = jnp.where(kept_mask, assigned * capacity + slot_rank, overflow)
    buffer = jnp.zeros((overflow, model_width), jnp.bfloat16)
    buffer = (
        buffer.at[slot_index[:tok_count]]
        .set(normed, mode="drop")
        .at[slot_index[tok_count:]]
        .set(normed, mode="drop")
    )
    first_matrix = w_in[0]
    bias_in_row = b_in[0]
    second_matrix = w_out[0]
    arrived = lax.all_to_all(
        buffer.reshape(expert_count, capacity, model_width),
        "expert",
        split_axis=0,
        concat_axis=0,
        tiled=True,
    )
    arrived = arrived.reshape(overflow, model_width)
    hidden = jnp.dot(
        lax.all_gather(arrived, "dp", axis=0, tiled=True),
        first_matrix,
        preferred_element_type=jnp.float32,
    )
    hidden = jnp.maximum(hidden + bias_in_row, 0.0).astype(jnp.bfloat16)
    partial_value = jnp.dot(hidden, second_matrix, preferred_element_type=jnp.float32).astype(
        jnp.bfloat16
    )
    summed = lax.psum(partial_value, "dp").astype(jnp.float32)
    summed = lax.dynamic_slice_in_dim(summed, lax.axis_index("dp") * overflow, overflow, 0)
    bias_out_row = lax.dynamic_slice_in_dim(b_out, lax.axis_index("expert"), 1, 0)
    results = (summed + bias_out_row).astype(jnp.bfloat16)
    returned = lax.all_to_all(
        results.reshape(expert_count, capacity, model_width),
        "expert",
        split_axis=0,
        concat_axis=0,
        tiled=True,
    )
    returned = returned.reshape(overflow, model_width)
    gate_values = gate_code.astype(jnp.float32) / 65536.0
    gate_flat = jnp.concatenate([gate_values[:, 0], gate_values[:, 1]])
    weights = jnp.where(kept_mask, gate_flat, 0.0)
    guard_index = jnp.minimum(slot_index, overflow - 1)
    picked = returned[guard_index].astype(jnp.float32) * weights[:, None]
    layer_out = hidden_state + picked[:tok_count] + picked[tok_count:]
    return layer_out.astype(jnp.bfloat16)


def solution(mesh):
    return jax.shard_map(
        per_device,
        mesh=mesh,
        in_specs=(
            P(("dp", "expert"), None),
            P(("dp", "expert"), None),
            P(("dp", "expert"), None),
            P(("dp", "expert"), None),
            P(("dp", "expert")),
            P(("dp", "expert"), None),
            P(("dp", "expert"), None),
            P(("dp", "expert"), None),
            P(),
            P(),
            P("expert", None, "dp"),
            P("expert", "dp"),
            P("expert", "dp", None),
            P(),
        ),
        out_specs=P(("dp", "expert"), None),
        check_vma=False,
    )
```

profile of v0, /device:TPU:8, one launch (start us, length us, event | category | flops | bytes accessed | tf_op | source)
XLA Modules:
  0.0 335.2 jit_solution(7050097430861302124)
XLA Ops:
  6.5 0.8 and_select_fusion.1
  7.7 1.0 scatter_custom_fusion
  8.7 0.7 all_to_all.22
  9.4 10.4 %all-to-all-start = ((s32[16,8,1]{1,2,0:T(1,128)}), s32[16,8,1]{1,2,0:T(1,128)S(1)}, u32[]{:S(2)}, u32[]{:S(2)}) async-start(s32[16,8,1]{1,2,0:T(1,128)} %bitcast), calls=%async_computation | async-start | bytes 16384 | tf_op jit(solution)/shard_map/all_to_all | solution.py:46
  19.8 6.0 %scatter_custom_fusion.1 = bf16[128,8192]{1,0:T(8,128)(2,1)} fusion(s32[128]{0:T(128)S(1)} %compare_select_fusion.4, bf16[128,2048]{1,0:T(8,128)(2,1)} %param.17, bf16[]{:T(256)} %constant.122, bf16[128,2048]{1,0:T(8,128)(2,1)} %param.16, bf16[128,2048]{1,0:T(8,128)(2,1)} %param.15, bf16[128,2048]{1,0:T(8,128)(2,1)} %param.14, bf16[]{:T(256)} %constant.46.clone.1), kind=kCustom, calls=%fused_computation.8 | custom fusion | flops 8388608 | bytes 4194308 | tf_op jit(solution)/shard_map/scatter | solution.py:42
  25.8 1.6 all-to-all-done
  27.4 5.8 %all-to-all-start.1 = ((bf16[16,8,8192]{2,1,0:T(8,128)(2,1)}), bf16[16,8,8192]{2,1,0:T(8,128)(2,1)}, u32[]{:S(2)}, u32[]{:S(2)}) async-start(bf16[16,8,8192]{2,1,0:T(8,128)(2,1)} %bitcast.2), calls=%async_computation.1 | async-start | bytes 4194304 | tf_op jit(solution)/shard_map/all_to_all | solution.py:45
  35.7 46.8 %all-to-all-done.1 = bf16[16,8,8192]{2,1,0:T(8,128)(2,1)} async-done(((bf16[16,8,8192]{2,1,0:T(8,128)(2,1)}), bf16[16,8,8192]{2,1,0:T(8,128)(2,1)}, u32[]{:S(2)}, u32[]{:S(2)}) %all-to-all-start.1) | async-done | bytes 2097184 | tf_op jit(solution)/shard_map/all_to_all | solution.py:45
  82.5 5.2 %scatter_custom_fusion.2 = bf16[128,8192]{1,0:T(8,128)(2,1)S(1)} fusion(s32[128]{0:T(128)S(1)} %fusion.32, bf16[16,8,8192]{2,1,0:T(8,128)(2,1)} %all-to-all-done.1, bf16[]{:T(256)} %constant.46.clone.1), kind=kCustom, calls=%fused_computation.16 | custom fusion | bytes 4194306 | tf_op jit(solution)/shard_map/scatter | solution.py:48
  87.7 1.3 fusion.39
  89.0 2.1 copy.28
  91.0 1.4 copy.29
  92.4 1.4 fusion.13
  94.3 1.4 fusion.22
  95.8 1.6 copy.33
  97.3 1.2 fusion.38
  98.6 1.3 multiply_reduce_fusion
  99.9 1.3 add_convert_fusion
  101.2 1.4 scatter_custom_fusion.3
  102.6 1.5 scatter_fusion
  104.3 22.6 %all_to_all.34 = bf16[32,2,2048]{2,1,0:T(2,128)(2,1)S(1)} all-to-all(bf16[32,2,2048]{2,1,0:T(2,128)(2,1)S(1)} %reshape.242), channel_id=1, replica_groups=mesh['dp'=16,'expert'=32] {'expert'}, dimensions={0} | all-to-all | bytes 524288 | tf_op jit(solution)/shard_map/all_to_all | solution.py:111
  126.9 0.8 reshape.243
  127.8 38.2 %all-gather.2.cloned.1.call-done = bf16[1024,2048]{1,0:T(8,128)(2,1)} async-done(((bf16[64,2048]{1,0:T(8,128)(2,1)}), bf16[1024,2048]{1,0:T(8,128)(2,1)}) %all-gather.2.cloned.1.call-update) | async-done | bytes 4194320 | tf_op jit(solution)/shard_map/all_gather | solution.py:120
  166.0 8.8 %convolution_convert_fusion = bf16[1024,2048]{1,0:T(8,128)(2,1)} fusion(bf16[1024,2048]{1,0:T(8,128)(2,1)} %all-gather.2.cloned.1.call-done, bf16[1,256,2048]{2,1,0:T(8,128)(2,1)S(1)} %copy-done, bf16[1,2048,256]{2,1,0:T(8,128)(2,1)} %param.24, f32[256]{0:T(256)S(1)} %bitcast.65), kind=kOutput, calls=%fused_computation.7 | convolution fusion | flops 2150367232 | bytes 10486784 | tf_op jit(solution)/shard_map/dot_general | solution.py:125
  175.5 0.9 constant_dynamic-slice_fusion
  176.3 124.8 %all-reduce.2.cloned.1.call-done = bf16[1024,2048]{1,0:T(8,128)(2,1)} async-done(((bf16[1024,2048]{1,0:T(8,128)(2,1)}), bf16[1024,2048]{1,0:T(8,128)(2,1)}) %all-reduce.2.cloned.1.call-update) | async-done | bytes 4194320 | tf_op jit(solution)/shard_map/psum | solution.py:128
  301.2 1.0 add_convert_fusion.1
  302.2 0.9 reshape.244
  303.0 9.8 %all-to-all-start.3 = ((bf16[32,2,2048]{2,1,0:T(2,128)(2,1)}), bf16[32,2,2048]{2,1,0:T(2,128)(2,1)S(1)}, u32[]{:S(2)}, u32[]{:S(2)}) async-start(bf16[32,2,2048]{2,1,0:T(2,128)(2,1)} %reshape.244), calls=%async_computation.3 | async-start | bytes 524288 | tf_op jit(solution)/shard_map/all_to_all | solution.py:132
  312.9 11.5 %all-to-all-done.3 = bf16[32,2,2048]{2,1,0:T(2,128)(2,1)S(1)} async-done(((bf16[32,2,2048]{2,1,0:T(2,128)(2,1)}), bf16[32,2,2048]{2,1,0:T(2,128)(2,1)S(1)}, u32[]{:S(2)}, u32[]{:S(2)}) %all-to-all-start.3) | async-done | bytes 262176 | tf_op jit(solution)/shard_map/all_to_all | solution.py:132
  324.6 1.4 gather_fusion
  326.1 2.2 fusion.16
  (53 shorter events, 4.6 us)
Async XLA Ops:
  6.5 159.5 %copy-start = (bf16[1,256,2048]{2,1,0:T(8,128)(2,1)S(1)}, bf16[1,256,2048]{2,1,0:T(8,128)(2,1)}, u32[]{:S(2)}) copy-start(bf16[1,256,2048]{2,1,0:T(8,128)(2,1)} %param.26) | copy-start | bytes 3145732
  9.4 18.0 %all-to-all-start = ((s32[16,8,1]{1,2,0:T(1,128)}), s32[16,8,1]{1,2,0:T(1,128)S(1)}, u32[]{:S(2)}, u32[]{:S(2)}) async-start(s32[16,8,1]{1,2,0:T(1,128)} %bitcast), calls=%async_computation | async-start | bytes 16384 | tf_op jit(solution)/shard_map/all_to_all | solution.py:46
  27.4 5.9 %copy-start.6 = (s32[128,2]{0,1:T(2,128)S(1)}, s32[128,2]{0,1:T(2,128)}, u32[]{:S(2)}) copy-start(s32[128,2]{0,1:T(2,128)} %param.20) | copy-start | bytes 3076
  27.4 6.9 %copy-start.5 = (s32[1,128]{1,0:T(1,128)S(1)}, s32[1,128]{1,0:T(1,128)}, u32[]{:S(2)}) copy-start(s32[1,128]{1,0:T(1,128)} %param.19) | copy-start | bytes 1540
  27.4 55.1 %all-to-all-start.1 = ((bf16[16,8,8192]{2,1,0:T(8,128)(2,1)}), bf16[16,8,8192]{2,1,0:T(8,128)(2,1)}, u32[]{:S(2)}, u32[]{:S(2)}) async-start(bf16[16,8,8192]{2,1,0:T(8,128)(2,1)} %bitcast.2), calls=%async_computation.1 | async-start | bytes 4194304 | tf_op jit(solution)/shard_map/all_to_all | solution.py:45
  33.2 132.8 %all-gather.2.cloned.1.call-start = ((), (), s32[]{:S(2)}) async-start(), calls=%async_computation.4 | async-start | bytes 4456448 | tf_op jit(solution)/shard_map/all_gather | solution.py:120
  87.7 3.3 copy-start.1
  91.0 3.0 copy-start.2
  97.3 2.6 copy-start.3
  97.3 2.6 copy-start.4
  102.6 63.4 %copy-start.8 = (f32[1,256]{1,0:T(1,128)S(1)}, f32[1,256]{1,0:T(1,128)}, u32[]{:S(2)}) copy-start(f32[1,256]{1,0:T(1,128)} %param.25) | copy-start | bytes 3076
  127.8 173.4 %all-reduce.2.cloned.1.call-start = ((), (), s32[]{:S(2)}) async-start(), calls=%async_computation.5 | async-start | bytes 8388608 | tf_op jit(solution)/shard_map/psum | solution.py:128
  174.8 0.7 copy-start.7
  303.0 21.4 %all-to-all-start.3 = ((bf16[32,2,2048]{2,1,0:T(2,128)(2,1)}), bf16[32,2,2048]{2,1,0:T(2,128)(2,1)S(1)}, u32[]{:S(2)}, u32[]{:S(2)}) async-start(bf16[32,2,2048]{2,1,0:T(2,128)(2,1)} %reshape.244), calls=%async_computation.3 | async-start | bytes 524288 | tf_op jit(solution)/shard_map/all_to_all | solution.py:132
Sparse Core Ops, SparseCore 0:
  127.9 38.0 all-gather.1
  174.9 126.1 all-reduce.1
where the time goes:
time: 336 us; the launch traced here: 335 us
  waiting for transfers between devices  223 us (66%)
  starting transfers between devices  26.2 us (8%)
  blocking collectives  22.6 us (7%)
  local copies, waits for them, and re-layouts  21.9 us (7%)
  other arithmetic  16.2 us (5%)
  between operations  13.7 us (4%)
  matrix products  11.6 us (3%)
    psum x1, waiting for transfers between devices, per_device(): summed = lax.psum(partial_value, 'dp').astype(jnp.float32)  125 us
    all_to_all x1, waiting for transfers between devices, per_device(): lax.all_to_all(send_rows, 'dp', split_axis=0, concat_axis=0, tiled=True)  46.8 us
    all_gather x1, waiting for transfers between devices, per_device(): lax.all_gather(arrived, 'dp', axis=0, tiled=True)  38.2 us
    all_to_all x1, blocking collectives, per_device(): lax.all_to_all(buffer.reshape(expert_count, capacity, model_width), 'expe...  22.6 us
    all_to_all x1, waiting for transfers between devices, per_device(): lax.all_to_all(results.reshape(expert_count, capacity, model_width), 'exp...  11.5 us
    all_to_all x1, starting transfers between devices, per_device(): lax.all_to_all(send_offsets, 'dp', split_axis=0, concat_axis=0, tiled=True)  10.4 us
    all_to_all x1, starting transfers between devices, per_device(): lax.all_to_all(results.reshape(expert_count, capacity, model_width), 'exp...  9.85 us
    dot_general x1, matrix products, per_device(): jnp.dot(hidden, second_matrix, preferred_element_type=jnp.float32)  8.76 us
  transfers between devices with their start and end apart: 5, of which 5 were waited for; matrix products, arithmetic and copies ran while one was open for 3% of the time, Pallas kernels for 0%

commit v1 on v0

--- a/solution.py
+++ b/solution.py
@@ -117,7 +117,9 @@
     )
     arrived = arrived.reshape(overflow, model_width)
     hidden = jnp.dot(
-        lax.all_gather(arrived, "dp", axis=0, tiled=True),
+        jnp.concatenate(
+            lax.all_to_all(jnp.stack([arrived] * lax.axis_size("dp")), "dp", 0, 0), axis=0
+        ),
         first_matrix,
         preferred_element_type=jnp.float32,
     )

time: 336 us -> 391 us (1.16)
  blocking collectives: 22.6 us -> 122 us
  waiting for transfers between devices: 223 us -> 179 us
    all_to_all x0 -> x1, blocking collectives: none -> 99.2 us  [per_device(): lax.all_to_all(jnp.stack([arrived] * lax.axis_size('dp')), 'dp', 0, 0)]
    all_gather x1 -> x0, waiting for transfers between devices: 38.2 us -> none  [per_device(): lax.all_gather(arrived, 'dp', axis=0, tiled=True)]
    psum x1, waiting for transfers between devices: 125 us -> 119 us  [per_device(): summed = lax.psum(partial_value, 'dp').astype(jnp.float32)]
  transfers between devices with their start and end apart: 5 -> 4, of which waited for: 5 -> 4; matrix products, arithmetic and copies ran while one was open for 3% -> 2% of each run, Pallas kernels for 0% -> 0%
where the time goes in v1:
time: 391 us; the launch traced here: 390 us
  waiting for transfers between devices  179 us (46%)
  blocking collectives  122 us (31%)
  starting transfers between devices  26.1 us (7%)
  local copies, waits for them, and re-layouts  21.7 us (6%)
  other arithmetic  16.2 us (4%)
  between operations  13.7 us (4%)
  matrix products  11.3 us (3%)
    psum x1, waiting for transfers between devices, per_device(): summed = lax.psum(partial_value, 'dp').astype(jnp.float32)  119 us
    all_to_all x1, blocking collectives, per_device(): lax.all_to_all(jnp.stack([arrived] * lax.axis_size('dp')), 'dp', 0, 0)  99.2 us
    all_to_all x1, waiting for transfers between devices, per_device(): lax.all_to_all(send_rows, 'dp', split_axis=0, concat_axis=0, tiled=True)  46.8 us
    all_to_all x1, blocking collectives, per_device(): lax.all_to_all(buffer.reshape(expert_count, capacity, model_width), 'expe...  22.6 us
    all_to_all x1, waiting for transfers between devices, per_device(): lax.all_to_all(results.reshape(expert_count, capacity, model_width), 'exp...  11.5 us
    all_to_all x1, starting transfers between devices, per_device(): lax.all_to_all(send_offsets, 'dp', split_axis=0, concat_axis=0, tiled=True)  10.4 us
    all_to_all x1, starting transfers between devices, per_device(): lax.all_to_all(results.reshape(expert_count, capacity, model_width), 'exp...  9.85 us
    dot_general x1, matrix products, per_device(): jnp.dot(hidden, second_matrix, preferred_element_type=jnp.float32)  8.46 us
  transfers between devices with their start and end apart: 4, of which 4 were waited for; matrix products, arithmetic and copies ran while one was open for 2% of the time, Pallas kernels for 0%

profile of v1, /device:TPU:8, one launch (start us, length us, event | category | flops | bytes accessed | tf_op | source)
XLA Modules:
  0.0 390.2 jit_solution(15437623915543173398)
XLA Ops:
  6.5 0.8 and_select_fusion.1
  7.7 1.0 scatter_custom_fusion
  8.7 0.7 all_to_all.25
  9.4 10.4 %all-to-all-start = ((s32[16,8,1]{1,2,0:T(1,128)}), s32[16,8,1]{1,2,0:T(1,128)S(1)}, u32[]{:S(2)}, u32[]{:S(2)}) async-start(s32[16,8,1]{1,2,0:T(1,128)} %bitcast), calls=%async_computation | async-start | bytes 16384 | tf_op jit(solution)/shard_map/all_to_all | solution.py:46
  19.8 6.0 %scatter_custom_fusion.1 = bf16[128,8192]{1,0:T(8,128)(2,1)} fusion(s32[128]{0:T(128)S(1)} %compare_select_fusion.4, bf16[128,2048]{1,0:T(8,128)(2,1)} %param.17, bf16[]{:T(256)} %constant.122, bf16[128,2048]{1,0:T(8,128)(2,1)} %param.16, bf16[128,2048]{1,0:T(8,128)(2,1)} %param.15, bf16[128,2048]{1,0:T(8,128)(2,1)} %param.14, bf16[]{:T(256)} %constant.46.clone.1), kind=kCustom, calls=%fused_computation.8 | custom fusion | flops 8388608 | bytes 4194308 | tf_op jit(solution)/shard_map/scatter | solution.py:42
  25.8 1.6 all-to-all-done
  27.4 5.8 %all-to-all-start.1 = ((bf16[16,8,8192]{2,1,0:T(8,128)(2,1)}), bf16[16,8,8192]{2,1,0:T(8,128)(2,1)}, u32[]{:S(2)}, u32[]{:S(2)}) async-start(bf16[16,8,8192]{2,1,0:T(8,128)(2,1)} %bitcast.2), calls=%async_computation.1 | async-start | bytes 4194304 | tf_op jit(solution)/shard_map/all_to_all | solution.py:45
  34.9 0.7 reduce.5
  35.7 46.8 %all-to-all-done.1 = bf16[16,8,8192]{2,1,0:T(8,128)(2,1)} async-done(((bf16[16,8,8192]{2,1,0:T(8,128)(2,1)}), bf16[16,8,8192]{2,1,0:T(8,128)(2,1)}, u32[]{:S(2)}, u32[]{:S(2)}) %all-to-all-start.1) | async-done | bytes 2097184 | tf_op jit(solution)/shard_map/all_to_all | solution.py:45
  82.5 5.2 %scatter_custom_fusion.2 = bf16[128,8192]{1,0:T(8,128)(2,1)S(1)} fusion(s32[128]{0:T(128)S(1)} %fusion.32, bf16[16,8,8192]{2,1,0:T(8,128)(2,1)} %all-to-all-done.1, bf16[]{:T(256)} %constant.46.clone.1), kind=kCustom, calls=%fused_computation.16 | custom fusion | bytes 4194306 | tf_op jit(solution)/shard_map/scatter | solution.py:48
  87.7 1.3 fusion.39
  89.0 2.1 copy.28
  91.0 1.4 copy.29
  92.4 1.4 fusion.13
  94.3 1.4 fusion.22
  95.8 1.6 copy.33
  97.3 1.2 fusion.38
  98.6 1.3 multiply_reduce_fusion
  99.9 1.3 add_convert_fusion
  101.2 1.4 scatter_custom_fusion.3
  102.6 1.5 scatter_fusion
  104.3 22.6 %all_to_all.39 = bf16[32,2,2048]{2,1,0:T(2,128)(2,1)S(1)} all-to-all(bf16[32,2,2048]{2,1,0:T(2,128)(2,1)S(1)} %reshape.244), channel_id=1, replica_groups=mesh['dp'=16,'expert'=32] {'expert'}, dimensions={0} | all-to-all | bytes 524288 | tf_op jit(solution)/shard_map/all_to_all | solution.py:111
  127.6 99.2 %all_to_all.40 = bf16[16,64,2048]{2,1,0:T(8,128)(2,1)} all-to-all(bf16[16,64,2048]{2,1,0:T(8,128)(2,1)S(1)} %stack.3), channel_id=1, replica_groups=mesh['dp'=16,'expert'=32] {'dp'}, dimensions={0} | all-to-all | bytes 8388608 | tf_op jit(solution)/shard_map/all_to_all | solution.py:121
  226.8 8.5 %convolution_convert_fusion = bf16[1024,2048]{1,0:T(8,128)(2,1)} fusion(bf16[1024,2048]{1,0:T(8,128)(2,1)} %bitcast.58, bf16[1,256,2048]{2,1,0:T(8,128)(2,1)S(1)} %copy-done, bf16[1,2048,256]{2,1,0:T(8,128)(2,1)S(1)} %copy-done.8, f32[256]{0:T(256)S(1)} %bitcast.67), kind=kOutput, calls=%fused_computation.7 | convolution fusion | flops 2150367232 | bytes 10486784 | tf_op jit(solution)/shard_map/dot_general | solution.py:127
  235.9 0.9 constant_dynamic-slice_fusion
  236.8 119.4 %all-reduce.2.cloned.1.call-done = bf16[1024,2048]{1,0:T(8,128)(2,1)} async-done(((bf16[1024,2048]{1,0:T(8,128)(2,1)}), bf16[1024,2048]{1,0:T(8,128)(2,1)}) %all-reduce.2.cloned.1.call-update) | async-done | bytes 4194320 | tf_op jit(solution)/shard_map/psum | solution.py:130
  356.2 1.0 add_convert_fusion.1
  357.2 0.9 reshape.246
  358.1 9.8 %all-to-all-start.4 = ((bf16[32,2,2048]{2,1,0:T(2,128)(2,1)}), bf16[32,2,2048]{2,1,0:T(2,128)(2,1)S(1)}, u32[]{:S(2)}, u32[]{:S(2)}) async-start(bf16[32,2,2048]{2,1,0:T(2,128)(2,1)} %reshape.246), calls=%async_computation.4 | async-start | bytes 524288 | tf_op jit(solution)/shard_map/all_to_all | solution.py:134
  368.0 11.5 %all-to-all-done.4 = bf16[32,2,2048]{2,1,0:T(2,128)(2,1)S(1)} async-done(((bf16[32,2,2048]{2,1,0:T(2,128)(2,1)}), bf16[32,2,2048]{2,1,0:T(2,128)(2,1)S(1)}, u32[]{:S(2)}, u32[]{:S(2)}) %all-to-all-start.4) | async-done | bytes 262176 | tf_op jit(solution)/shard_map/all_to_all | solution.py:134
  379.6 1.4 gather_fusion
  381.2 2.2 fusion.16
  (54 shorter events, 4.5 us)
Async XLA Ops:
  6.5 220.2 %copy-start = (bf16[1,256,2048]{2,1,0:T(8,128)(2,1)S(1)}, bf16[1,256,2048]{2,1,0:T(8,128)(2,1)}, u32[]{:S(2)}) copy-start(bf16[1,256,2048]{2,1,0:T(8,128)(2,1)} %param.26) | copy-start | bytes 3145732
  9.4 18.0 %all-to-all-start = ((s32[16,8,1]{1,2,0:T(1,128)}), s32[16,8,1]{1,2,0:T(1,128)S(1)}, u32[]{:S(2)}, u32[]{:S(2)}) async-start(s32[16,8,1]{1,2,0:T(1,128)} %bitcast), calls=%async_computation | async-start | bytes 16384 | tf_op jit(solution)/shard_map/all_to_all | solution.py:46
  27.4 5.9 %copy-start.6 = (s32[128,2]{0,1:T(2,128)S(1)}, s32[128,2]{0,1:T(2,128)}, u32[]{:S(2)}) copy-start(s32[128,2]{0,1:T(2,128)} %param.20) | copy-start | bytes 3076
  27.4 6.9 %copy-start.5 = (s32[1,128]{1,0:T(1,128)S(1)}, s32[1,128]{1,0:T(1,128)}, u32[]{:S(2)}) copy-start(s32[1,128]{1,0:T(1,128)} %param.19) | copy-start | bytes 1540
  27.4 55.1 %all-to-all-start.1 = ((bf16[16,8,8192]{2,1,0:T(8,128)(2,1)}), bf16[16,8,8192]{2,1,0:T(8,128)(2,1)}, u32[]{:S(2)}, u32[]{:S(2)}) async-start(bf16[16,8,8192]{2,1,0:T(8,128)(2,1)} %bitcast.2), calls=%async_computation.1 | async-start | bytes 4194304 | tf_op jit(solution)/shard_map/all_to_all | solution.py:45
  33.2 322.9 %all-reduce.2.cloned.1.call-start = ((), (), s32[]{:S(2)}) async-start(), calls=%async_computation.5 | async-start | bytes 8388608 | tf_op jit(solution)/shard_map/psum | solution.py:130
  87.7 3.3 copy-start.1
  91.0 3.0 copy-start.2
  97.3 2.6 copy-start.3
  97.3 2.6 copy-start.4
  127.6 99.2 %copy-start.8 = (bf16[1,2048,256]{2,1,0:T(8,128)(2,1)S(1)}, bf16[1,2048,256]{2,1,0:T(8,128)(2,1)}, u32[]{:S(2)}) copy-start(bf16[1,2048,256]{2,1,0:T(8,128)(2,1)} %param.24) | copy-start | bytes 3145732
  127.6 99.2 %copy-start.9 = (f32[1,256]{1,0:T(1,128)S(1)}, f32[1,256]{1,0:T(1,128)}, u32[]{:S(2)}) copy-start(f32[1,256]{1,0:T(1,128)} %param.25) | copy-start | bytes 3076
  235.2 0.7 copy-start.7
  358.1 21.4 %all-to-all-start.4 = ((bf16[32,2,2048]{2,1,0:T(2,128)(2,1)}), bf16[32,2,2048]{2,1,0:T(2,128)(2,1)S(1)}, u32[]{:S(2)}, u32[]{:S(2)}) async-start(bf16[32,2,2048]{2,1,0:T(2,128)(2,1)} %reshape.246), calls=%async_computation.4 | async-start | bytes 524288 | tf_op jit(solution)/shard_map/all_to_all | solution.py:134
Sparse Core Ops, SparseCore 0:
  235.4 120.7 all-reduce.1
